TPU v7x, 32 devices: a whole 2x2x4 slice. The times are simulated.
32 devices in a mesh: cells: 8 (over z, x), genes: 4 (over y, core).
Axes of the slice: x: 2, y: 2, z: 4, core: 2. Of those that a mesh axis runs over, the one named last changes fastest.
Arguments:
- counts: bfloat16 [8192, 13500], P('cells', 'genes'), may hold values from 0.0099487305 to 200
- library: int32 [8192], P('cells'), may hold values from 1000 to 20000
- cell_mask: int32 [8192], P('cells'), may hold values 0 or 1
- slide_len: int32 [3], replicated, may hold values from 1 to 4096, 8192 in all
- kl_step: int32 [1], replicated, may hold values from 0 to 1999
- noise: bfloat16 [8192, 512], P('cells'), may hold values from -5 to 5
- emb_weight: bfloat16 [1024, 13500], P(None, 'genes'), may hold values from -0.0546875 to 0.0546875
- ln_gain: float32 [1024], replicated, may hold values from 0.5 to 1.5
- ln_bias: float32 [1024], replicated, may hold values from -1.5 to 1.5
- lat_weight: bfloat16 [1024, 1024], replicated, may hold values from -0.1875 to 0.1875
- lat_bias: float32 [1024], replicated, may hold values from -2 to 2
- up_weight: bfloat16 [1024, 512], replicated, may hold values from -0.25 to 0.25
- dec_weight: bfloat16 [1024, 13500], P(None, 'genes'), may hold values from -0.1875 to 0.1875
- prior_mean: float32 [512, 16], replicated, may hold values from -4 to 4
- prior_logvar: float32 [512, 16], replicated, may hold values from -1 to 1
- out_grad: bfloat16 [8192, 13500], P('cells', 'genes'), may hold values from -6 to 6
Outputs:
- decoded: bfloat16 [8192, 13500], P('cells', 'genes')
- counts_grad: bfloat16 [8192, 13500], P('cells', 'genes')
- emb_weight_grad: float32 [1024, 13500], P('cells', 'genes')
- ln_gain_grad: float32 [1024], P('cells')
- ln_bias_grad: float32 [1024], P('cells')
- lat_weight_grad: float32 [1024, 1024], P('cells')
- lat_bias_grad: float32 [1024], P('cells')
- up_weight_grad: float32 [1024, 512], P('cells')
- dec_weight_grad: float32 [1024, 13500], P('cells', 'genes')
- prior_mean_grad: float32 [512, 16], P('cells')
- prior_logvar_grad: float32 [512, 16], P('cells')
- kl_loss: float32 [1], replicated
Inputs may be any that keep to these rules, and one draw needn't show every extreme that they name: `slide_len`: slide lengths sum to 8192.
All inputs are finite; a program needn't handle non-finite values. No bound on the sum of `cell_mask` on one device may be relied on, other than what follows from the above.
Results may differ from a plain program's by a relative error of at most 0.009.
Values may be sent and summed in bfloat16 or wider, within the bound.
A program may use at most 192 MiB of HBM per device.

v0:
```python
import jax
import jax.numpy as jnp
from jax import lax
from jax.sharding import PartitionSpec as P

WARM = 1000
epsilon = 1e-05
free_bits = 1.0


def exact_dot(left, right):
    return jnp.dot(left, right, precision=lax.Precision.HIGHEST, preferred_element_type=jnp.float32)


def exact_tdot(left, right):
    return lax.dot_general(
        left,
        right,
        (((0,), (0,)), ((), ())),
        precision=lax.Precision.HIGHEST,
        preferred_element_type=jnp.float32,
    )


def half_dot(left, right):
    return jnp.dot(left, right, preferred_element_type=jnp.float32)


def half_tdot(left, right):
    return lax.dot_general(
        left, right, (((0,), (0,)), ((), ())), preferred_element_type=jnp.float32
    )


def half_ntdot(left, right):
    return lax.dot_general(
        left, right, (((1,), (1,)), ((), ())), preferred_element_type=jnp.float32
    )


def bottleneck_forward(
    embedded, noise_rows, ln_gain, ln_bias, lat_weight, lat_bias, up_weight, tables
):
    prec_tab, mean_prec, const_tab = tables
    latent_w = up_weight.shape[1]
    centred = embedded - jnp.mean(embedded, -1, keepdims=True)
    inv_dev = lax.rsqrt(jnp.mean(centred * centred, -1, keepdims=True) + epsilon)
    normal = centred * inv_dev
    hidden = normal * ln_gain + ln_bias
    hidden_low = hidden.astype(jnp.bfloat16)
    latent = half_dot(hidden_low, lat_weight) + lat_bias
    lat_mean = latent[:, :latent_w]
    log_var = latent[:, latent_w:]
    variance = jnp.exp(log_var)
    spread = jnp.exp(0.5 * log_var)
    sample_low = (lat_mean + spread * noise_rows.astype(jnp.float32)).astype(jnp.bfloat16)
    mixed_low = (hidden + half_ntdot(sample_low, up_weight)).astype(jnp.bfloat16)
    logits = -0.5 * (
        exact_dot(lat_mean * lat_mean, prec_tab)
        - 2.0 * exact_dot(lat_mean, mean_prec)
        + jnp.sum(const_tab, 0)
    )
    resp = jax.nn.softmax(logits * latent_w ** (-0.5), axis=-1)
    resp_prec = exact_dot(resp, prec_tab.T)
    resp_mean = exact_dot(resp, mean_prec.T)
    diverge = 0.5 * (
        exact_dot(resp, const_tab.T)
        - log_var
        + (variance + lat_mean * lat_mean) * resp_prec
        - 2.0 * lat_mean * resp_mean
        - 1.0
    )
    kept = (
        normal,
        inv_dev,
        hidden_low,
        lat_mean,
        log_var,
        variance,
        spread,
        sample_low,
        resp,
        resp_prec,
        resp_mean,
    )
    return (mixed_low, diverge, kept)


def bottleneck_backward(
    mixed_grad, weight, noise_rows, kept, ln_gain, lat_weight, up_weight, prior_mean, tables
):
    prec_tab, mean_prec, const_tab = tables
    (
        normal,
        inv_dev,
        hidden_low,
        lat_mean,
        log_var,
        variance,
        spread,
        sample_low,
        resp,
        resp_prec,
        resp_mean,
    ) = kept
    latent_w = up_weight.shape[1]
    up_grad = half_tdot(mixed_grad, sample_low)
    sample_grad = half_dot(mixed_grad, up_weight)
    mean_grad = sample_grad + weight * (lat_mean * resp_prec - resp_mean)
    var_grad = sample_grad * 0.5 * spread * noise_rows.astype(jnp.float32) + 0.5 * weight * (
        variance * resp_prec - 1.0
    )
    moment = variance + lat_mean * lat_mean
    resp_grad = 0.5 * (
        exact_dot(weight, const_tab)
        + exact_dot(weight * moment, prec_tab)
        - 2.0 * exact_dot(weight * lat_mean, mean_prec)
    )
    logit_grad = (
        resp * (resp_grad - jnp.sum(resp * resp_grad, -1, keepdims=True)) * latent_w ** (-0.5)
    )
    mean_grad = (
        mean_grad
        - lat_mean * exact_dot(logit_grad, prec_tab.T)
        + exact_dot(logit_grad, mean_prec.T)
    )
    const_grad = 0.5 * exact_tdot(weight, resp) - 0.5 * jnp.sum(logit_grad, 0)[None, :]
    mprec_grad = -exact_tdot(weight * lat_mean, resp) + exact_tdot(lat_mean, logit_grad)
    prec_grad = (
        0.5 * exact_tdot(weight * moment, resp)
        - 0.5 * exact_tdot(lat_mean * lat_mean, logit_grad)
        + prior_mean * prior_mean * const_grad
        + prior_mean * mprec_grad
    )
    pmean_grad = 2.0 * prior_mean * prec_tab * const_grad + prec_tab * mprec_grad
    plogv_grad = const_grad - prec_tab * prec_grad
    latent_grad = jnp.concatenate([mean_grad, var_grad], axis=1).astype(jnp.bfloat16)
    latb_grad = jnp.sum(latent_grad.astype(jnp.float32), 0)
    latw_grad = half_tdot(hidden_low, latent_grad)
    hidden_grad = mixed_grad.astype(jnp.float32) + half_ntdot(latent_grad, lat_weight)
    gain_grad = jnp.sum(hidden_grad * normal, 0)
    shift_grad = jnp.sum(hidden_grad, 0)
    normal_grad = hidden_grad * ln_gain
    embed_grad = inv_dev * (
        normal_grad
        - jnp.mean(normal_grad, -1, keepdims=True)
        - normal * jnp.mean(normal_grad * normal, -1, keepdims=True)
    )
    small = (latw_grad, up_grad, gain_grad, shift_grad, latb_grad, pmean_grad, plogv_grad)
    return (embed_grad.astype(jnp.bfloat16), small)


def on_device(
    counts,
    library,
    cell_mask,
    slide_len,
    kl_step,
    noise,
    emb_weight,
    ln_gain,
    ln_bias,
    lat_weight,
    lat_bias,
    up_weight,
    dec_weight,
    prior_mean,
    prior_logvar,
    out_grad,
):
    rows = counts.shape[0]
    first = lax.axis_index("cells") * rows
    place = first + jnp.arange(rows, dtype=jnp.int32)
    ends = jnp.cumsum(slide_len)
    slide_of = jnp.sum((ends[None, :] <= place[:, None]).astype(jnp.int32), 1)
    onehot = (slide_of[:, None] == jnp.arange(slide_len.shape[0], dtype=jnp.int32)[None, :]).astype(
        jnp.float32
    )
    live = cell_mask.astype(jnp.float32)
    libsize = library.astype(jnp.float32)
    lib_total, live_total = lax.psum(
        (jnp.sum(onehot * (libsize * live)[:, None], 0), jnp.sum(onehot * live[:, None], 0)),
        "cells",
    )
    slide_lib = lib_total / jnp.maximum(live_total, 1.0)
    scale = jnp.sum(onehot * slide_lib[None, :], 1) / libsize
    total = jnp.maximum(jnp.sum(live_total), 1.0)
    beta = jnp.minimum(1.0, kl_step[0].astype(jnp.float32) / WARM)
    prec_tab = jnp.exp(-prior_logvar)
    tables = (prec_tab, prior_mean * prec_tab, prior_mean * prior_mean * prec_tab + prior_logvar)
    counts_f = counts.astype(jnp.float32)
    normed_low = jnp.log1p(counts_f * scale[:, None]).astype(jnp.bfloat16)
    partial_embed = half_ntdot(normed_low, emb_weight)
    embedded = lax.psum(partial_embed, "genes")
    mixed_low, diverge, kept = bottleneck_forward(
        embedded, noise, ln_gain, ln_bias, lat_weight, lat_bias, up_weight, tables
    )
    kl_sum = lax.psum(jnp.sum(diverge * live[:, None], 0), "cells")
    decoded = half_dot(mixed_low, dec_weight).astype(jnp.bfloat16)
    average = kl_sum / total
    kl_loss = beta * jnp.sum(jnp.maximum(average, free_bits))
    active = (average > free_bits).astype(jnp.float32)
    partial_mixed = half_ntdot(out_grad, dec_weight)
    dec_grad = half_tdot(mixed_low, out_grad)
    weight_rows = beta * active[None, :] * live[:, None] / total
    mixed_grad = lax.psum(partial_mixed, "genes").astype(jnp.bfloat16)
    embed_grad, small = bottleneck_backward(
        mixed_grad, weight_rows, noise, kept, ln_gain, lat_weight, up_weight, prior_mean, tables
    )
    normed_grad = half_dot(embed_grad, emb_weight)
    counts_grad = (normed_grad * scale[:, None] / (1.0 + counts_f * scale[:, None])).astype(
        jnp.bfloat16
    )
    latw_grad, up_grad, gain_grad, shift_grad, latb_grad, pmean_grad, plogv_grad = small
    emb_grad = half_tdot(embed_grad, normed_low)
    summed = (
        lax.psum_scatter(emb_grad, "cells", scatter_dimension=0, tiled=True),
        lax.psum_scatter(dec_grad, "cells", scatter_dimension=0, tiled=True),
        lax.psum_scatter(latw_grad, "cells", scatter_dimension=0, tiled=True),
        lax.psum_scatter(up_grad, "cells", scatter_dimension=0, tiled=True),
        lax.psum_scatter(gain_grad, "cells", scatter_dimension=0, tiled=True),
        lax.psum_scatter(shift_grad, "cells", scatter_dimension=0, tiled=True),
        lax.psum_scatter(latb_grad, "cells", scatter_dimension=0, tiled=True),
        lax.psum_scatter(pmean_grad, "cells", scatter_dimension=0, tiled=True),
        lax.psum_scatter(plogv_grad, "cells", scatter_dimension=0, tiled=True),
    )
    emb_out, dec_out, latw_out, up_out, gain_out, shift_out, latb_out, pmean_out, plogv_out = summed
    return (
        decoded,
        counts_grad,
        emb_out,
        gain_out,
        shift_out,
        latw_out,
        latb_out,
        up_out,
        dec_out,
        pmean_out,
        plogv_out,
        kl_loss.reshape(1),
    )


def solution(mesh):
    placed = (
        P("cells", "genes"),
        P("cells"),
        P("cells"),
        P(),
        P(),
        P("cells", None),
        P(None, "genes"),
        P(),
        P(),
        P(),
        P(),
        P(),
        P(None, "genes"),
        P(),
        P(),
        P("cells", "genes"),
    )
    return jax.shard_map(
        on_device,
        mesh=mesh,
        in_specs=placed,
        out_specs=(
            P("cells", "genes"),
            P("cells", "genes"),
            P("cells", "genes"),
            P("cells"),
            P("cells"),
            P("cells", None),
            P("cells"),
            P("cells", None),
            P("cells", "genes"),
            P("cells", None),
            P("cells", None),
            P(),
        ),
        check_vma=False,
    )
```

profile of v0, /device:TPU:0, one launch (start us, length us, event | category | flops | bytes accessed | tf_op | source)
XLA Modules:
  0.0 957.3 jit_solution(9360086987290301371)
XLA Ops:
  7.2 0.8 convert_element_type.56
  8.1 0.7 broadcast_multiply_fusion
  8.8 0.8 reduce-window.8
  9.7 0.2 select_reduce_fusion.1
  9.8 23.1 %all-reduce.4 = (f32[3]{0:T(128)S(1)}, f32[3]{0:T(128)S(1)}) all-reduce(f32[3]{0:T(128)S(1)} %get-tuple-element.17, f32[3]{0:T(128)S(1)} %get-tuple-element.16), channel_id=1, replica_groups=mesh['cells'=8,'genes'=4] {'cells'}, use_global_device_ids=true, to_apply=%region_3.4 | all-reduce | flops 6 | bytes 48 | tf_op jit(solution)/shard_map/psum | solution.py:181
  33.0 0.6 fusion.62
  33.7 0.7 convert_divide_fusion
  34.4 14.0 %fusion.1 = f32[1024,1024]{1,0:T(8,128)} fusion(bf16[1024,3375]{0,1:T(8,128)(2,1)} %param.22, bf16[1024,3375]{0,1:T(8,128)(2,1)} %param.16, f32[1024]{0:T(1024)S(1)} %convert_divide_fusion), kind=kOutput, calls=%fused_computation.5 | convolution fusion | flops 7088256000 | bytes 18022400 | tf_op jit(solution)/shard_map/dot_general | solution.py:36
  49.1 14.3 %fusion.64 = f32[1024,1024]{1,0:T(8,128)} fusion(bf16[1024,3375]{0,1:T(8,128)(2,1)} %param.31, bf16[1024,3375]{0,1:T(8,128)(2,1)} %param.28), kind=kOutput, calls=%fused_computation.101 | convolution fusion | flops 7077888000 | bytes 18018304 | tf_op jit(solution)/shard_map/dot_general | solution.py:36
  64.3 67.0 %all-reduce.8.cloned.1.call-done = f32[1024,1024]{1,0:T(8,128)} async-done(((f32[1024,1024]{1,0:T(8,128)}), f32[1024,1024]{1,0:T(8,128)}) %all-reduce.8.cloned.1.call-update) | async-done | bytes 4194320 | tf_op jit(solution)/shard_map/psum | solution.py:194
  131.3 2.4 reduce_sum.166
  133.8 2.9 multiply_reduce_fusion.2
  136.7 0.5 copy-done.2
  137.2 2.5 broadcast_add_fusion
  139.7 1.9 convolution_multiply_fusion.1
  141.6 2.0 fusion.63
  143.6 1.8 fusion.55
  145.4 1.9 fusion.41
  147.3 1.3 copy-done.10
  148.6 2.7 multiply_reduce_fusion.4
  151.4 21.8 %psum.39 = f32[512]{0:T(512)S(1)} all-reduce(f32[512]{0:T(512)S(1)} %multiply_reduce_fusion.4), channel_id=1, replica_groups=mesh['cells'=8,'genes'=4] {'cells'}, use_global_device_ids=true, to_apply=%region_15.16 | all-reduce | flops 512 | bytes 4096 | tf_op jit(solution)/shard_map/psum | solution.py:198
  173.1 0.6 maximum_reduce_fusion
  173.7 2.0 fusion.36
  175.8 1.5 convolution_negate_fusion
  177.3 2.3 convolution_add_fusion
  179.6 2.2 multiply_reduce_fusion.5
  181.8 0.1 fusion.61
  181.9 1.4 fusion.26
  183.3 1.3 fusion.23
  184.6 1.2 multiply_add_fusion.1
  185.8 1.7 fusion.31
  187.5 0.8 copy.45
  188.5 76.6 %all-reduce.9 = bf16[1024,1024]{1,0:T(8,128)(2,1)} all-reduce(f32[1024,1024]{1,0:T(8,128)} %fusion.64), channel_id=1, replica_groups=mesh['cells'=8,'genes'=4] {'genes'}, use_global_device_ids=true, to_apply=%region_10.11 | all-reduce | flops 1048576 | bytes 6291456 | tf_op jit(solution)/shard_map/psum | solution.py:206
  265.1 0.8 copy.43
  266.0 7.7 fusion.6
  273.7 1.0 copy-done.20
  274.7 2.7 fusion.66
  277.5 1.8 fusion.40
  279.3 6.0 add_convert_fusion.1
  285.4 1.0 copy-done.11
  286.4 4.5 fusion.37
  290.9 0.3 reduce-scatter.11.cloned.1.call-start
  291.2 8.4 multiply_reduce_fusion
  299.5 19.0 %fusion = f32[1024,3375]{0,1:T(8,128)} fusion(bf16[1024,3375]{0,1:T(8,128)(2,1)} %param.16, f32[1024]{0:T(1024)S(1)} %convert_divide_fusion, f32[1024,1024]{1,0:T(8,128)} %get-tuple-element.40, f32[1024,1024]{1,0:T(8,128)S(1)} %copy-done.4, f32[1024]{0:T(1024)S(1)} %get-tuple-element.43, f32[1024]{0:T(1024)S(1)} %get-tuple-element.44, ...), kind=kOutput, calls=%fused_computation.4 | convolution fusion | flops 7096644608 | bytes 29149184 | tf_op jit(solution)/shard_map/dot_general | solution.py:30
  318.6 0.3 reduce-scatter.17.cloned.1.call-start
  318.9 0.9 copy-done.15
  319.8 0.3 copy-done.21
  320.1 3.6 add_convert_fusion
  323.7 1.3 copy-done.22
  325.0 13.4 %fusion.65 = f32[1024,3375]{0,1:T(8,128)} fusion(bf16[1024,1024]{1,0:T(8,128)(2,1)S(1)} %add_convert_fusion, bf16[1024,3375]{0,1:T(8,128)(2,1)} %param.31), kind=kOutput, calls=%fused_computation.102 | convolution fusion | flops 7077888000 | bytes 22833152 | tf_op jit(solution)/shard_map/dot_general | solution.py:30
  338.5 0.6 copy-done.19
  339.1 0.6 dynamic-slice
  340.3 0.4 convert_reduce_fusion
  340.7 33.7 %all-reduce.3 = (f32[1024]{0:T(1024)S(1)}, f32[1024]{0:T(1024)S(1)}, f32[1024]{0:T(1024)S(1)}) all-reduce(f32[1024]{0:T(1024)S(1)} %get-tuple-element.12, f32[1024]{0:T(1024)S(1)} %get-tuple-element.15, f32[1024]{0:T(1024)S(1)} %convert_reduce_fusion), channel_id=3, replica_groups=mesh['cells'=8,'genes'=4] {'cells'}, use_global_device_ids=true, to_apply=%region_22.23.clone | all-reduce | flops 3072 | bytes 24576
  374.4 0.6 dynamic-slice.1
  375.0 0.6 dynamic-slice.3
  375.6 0.6 dynamic-slice.5
  376.8 12.2 %convolution_convert_fusion = bf16[1024,3375]{0,1:T(8,128)(2,1)} fusion(bf16[1024,1024]{1,0:T(8,128)(2,1)} %copy-done.22, bf16[1024,3375]{0,1:T(8,128)(2,1)} %param.28), kind=kOutput, calls=%fused_computation.3 | convolution fusion | flops 7081344000 | bytes 15921152 | tf_op jit(solution)/shard_map/dot_general | solution.py:26
  389.0 16.2 %divide_convert_fusion = bf16[1024,3375]{0,1:T(8,128)(2,1)} fusion(bf16[1024,3375]{0,1:T(8,128)(2,1)} %param.16, bf16[1024,3375]{0,1:T(8,128)(2,1)} %param.22, f32[1024]{0:T(1024)S(1)} %convert_divide_fusion, f32[1024,1024]{1,0:T(8,128)S(1)} %copy-done.23, f32[1024,1024]{1,0:T(8,128)S(1)} %copy-done.5, f32[1024]{0:T(1024)S(1)} %get-tuple-element.43, ...), kind=kOutput, calls=%fused_computation | convolution fusion | flops 7107012608 | bytes 29149184 | tf_op jit(solution)/shard_map/dot_general | solution.py:26
  405.2 1.4 copy.46
  406.6 1.4 copy.44
  408.0 79.9 %reduce-scatter.13.cloned.1.call-done = f32[128,1024]{1,0:T(8,128)} async-done(((f32[1024,1024]{1,0:T(8,128)}), f32[128,1024]{1,0:T(8,128)}) %reduce-scatter.13.cloned.1.call-update) | async-done | bytes 524304 | tf_op jit(solution)/shard_map/reduce_scatter | solution.py:219
  487.9 230.7 %reduce-scatter.11.cloned.1.call-done = f32[128,3375]{0,1:T(8,128)} async-done(((f32[1024,3375]{0,1:T(8,128)}), f32[128,3375]{0,1:T(8,128)}) %reduce-scatter.11.cloned.1.call-update) | async-done | bytes 1728016 | tf_op jit(solution)/shard_map/reduce_scatter | solution.py:217
  718.6 230.2 %reduce-scatter.17.cloned.1.call-done = f32[128,3375]{0,1:T(8,128)} async-done(((f32[1024,3375]{0,1:T(8,128)}), f32[128,3375]{0,1:T(8,128)}) %reduce-scatter.17.cloned.1.call-update) | async-done | bytes 1728016 | tf_op jit(solution)/shard_map/reduce_scatter | solution.py:218
  (64 shorter events, 0.8 us)
Async XLA Ops:
  7.2 129.5 %copy-start = (bf16[1024,1024]{1,0:T(8,128)(2,1)S(1)}, bf16[1024,1024]{1,0:T(8,128)(2,1)}, u32[]{:S(2)}) copy-start(bf16[1024,1024]{1,0:T(8,128)(2,1)} %param.25) | copy-start | bytes 6291460
  7.2 124.1 %all-reduce.8.cloned.1.call-start = ((), (), s32[]{:S(2)}) async-start(), calls=%async_computation.6 | async-start | bytes 8388608 | tf_op jit(solution)/shard_map/psum | solution.py:194
  48.4 356.8 %reduce-scatter.21.cloned.1.call-start = ((), (), s32[]{:S(2)}) async-start(), calls=%async_computation.12 | async-start | bytes 294912
  49.1 15.0 %copy-start.13 = (f32[512,16]{0,1:T(8,128)S(1)}, f32[512,16]{0,1:T(8,128)}, u32[]{:S(2)}) copy-start(f32[512,16]{0,1:T(8,128)} %param.30) | copy-start | bytes 98308
  49.1 15.0 %copy-start.14 = (f32[512,16]{0,1:T(8,128)S(1)}, f32[512,16]{0,1:T(8,128)}, u32[]{:S(2)}) copy-start(f32[512,16]{0,1:T(8,128)} %param.29) | copy-start | bytes 98308
  64.3 72.5 %copy-start.16 = (f32[1024]{0:T(1024)S(1)}, f32[1024]{0:T(1024)}, u32[]{:S(2)}) copy-start(f32[1024]{0:T(1024)} %param.26) | copy-start | bytes 12292
  64.3 72.5 %copy-start.17 = (f32[1024]{0:T(1024)S(1)}, f32[1024]{0:T(1024)}, u32[]{:S(2)}) copy-start(f32[1024]{0:T(1024)} %param.24) | copy-start | bytes 12292
  64.3 72.5 %copy-start.18 = (f32[1024]{0:T(1024)S(1)}, f32[1024]{0:T(1024)}, u32[]{:S(2)}) copy-start(f32[1024]{0:T(1024)} %param.23) | copy-start | bytes 12292
  133.8 3.5 copy-start.2
  139.7 7.6 copy-start.6
  145.4 1.9 copy-start.9
  147.3 1.3 copy-start.10
  173.1 2.7 copy-start.7
  188.4 218.2 %reduce-scatter.19.cloned.1.call-start = ((), (), s32[]{:S(2)}) async-start(), calls=%async_computation.11 | async-start | bytes 294912
  265.9 142.1 %reduce-scatter.15.cloned.1.call-start = ((), (), s32[]{:S(2)}) async-start(), calls=%async_computation.9 | async-start | bytes 2359296 | tf_op jit(solution)/shard_map/reduce_scatter | solution.py:220
  266.0 8.7 copy-start.8
  273.7 1.0 copy-start.20
  277.4 210.5 %reduce-scatter.13.cloned.1.call-start = ((), (), s32[]{:S(2)}) async-start(), calls=%async_computation.8 | async-start | bytes 4718592 | tf_op jit(solution)/shard_map/reduce_scatter | solution.py:219
  279.3 7.0 copy-start.3
  285.4 1.0 copy-start.11
  290.9 427.7 %reduce-scatter.11.cloned.1.call-start = ((), (), s32[]{:S(2)}) async-start(), calls=%async_computation.7 | async-start | bytes 15556608 | tf_op jit(solution)/shard_map/reduce_scatter | solution.py:217
  291.2 8.4 copy-start.4
  318.5 1.2 copy-start.15
  318.5 1.5 copy-start.21
  318.6 630.3 %reduce-scatter.17.cloned.1.call-start = ((), (), s32[]{:S(2)}) async-start(), calls=%async_computation.10 | async-start | bytes 15556608 | tf_op jit(solution)/shard_map/reduce_scatter | solution.py:218
  323.7 1.3 copy-start.22
  338.4 0.7 copy-start.19
  338.4 1.9 copy-start.12
  376.8 12.2 %copy-start.5 = (f32[1024,1024]{1,0:T(8,128)S(1)}, f32[1024,1024]{1,0:T(8,128)}, u32[]{:S(2)}) copy-start(f32[1024,1024]{1,0:T(8,128)} %all-reduce.8.cloned.1.call-done) | copy-start | bytes 12582916
  376.8 12.2 %copy-start.23 = (f32[1024,1024]{1,0:T(8,128)S(1)}, f32[1024,1024]{1,0:T(8,128)}, u32[]{:S(2)}) copy-start(f32[1024,1024]{1,0:T(8,128)} %get-tuple-element.40) | copy-start | bytes 12582916
  389.0 559.8 %copy-start.1 = (bf16[1024,1024]{1,0:T(8,128)(2,1)S(1)}, bf16[1024,1024]{1,0:T(8,128)(2,1)}, u32[]{:S(2)}) copy-start(bf16[1024,1024]{1,0:T(8,128)(2,1)} %param.25) | copy-start | bytes 6291460
Sparse Core Ops, SparseCore 0:
  48.5 82.7 all-reduce.7
  188.5 58.4 reduce-scatter.20
  266.1 58.3 reduce-scatter.18
  328.4 68.1 reduce-scatter.14
  400.6 87.2 reduce-scatter.12
  491.9 226.6 reduce-scatter.10
  722.7 226.0 reduce-scatter.16
where the time goes:
time: 963 us; the launch traced here: 957 us
  waiting for transfers between devices  608 us (63%)
  blocking collectives  155 us (16%)
  matrix products  150 us (16%)
  between operations  18.7 us (2%)
  local copies, waits for them, and re-layouts  13.8 us (1%)
  other arithmetic  10.6 us (1%)
    reduce_scatter x1, waiting for transfers between devices, on_device(): lax.psum_scatter(emb_grad, 'cells', scatter_dimension=0, tiled=True)  231 us
    reduce_scatter x1, waiting for transfers between devices, on_device(): lax.psum_scatter(dec_grad, 'cells', scatter_dimension=0, tiled=True)  230 us
    reduce_scatter x1, waiting for transfers between devices, on_device(): lax.psum_scatter(latw_grad, 'cells', scatter_dimension=0, tiled=True)  79.9 us
    psum x1, blocking collectives, on_device(): mixed_grad = lax.psum(partial_mixed, 'genes').astype(jnp.bfloat16)  76.6 us
    psum x1, waiting for transfers between devices, on_device(): embedded = lax.psum(partial_embed, 'genes')  67 us
    dot_general x4, matrix products, half_ntdot(): lax.dot_general(left, right, (((1,), (1,)), ((), ())), preferred_element_...  40.3 us
    dot_general x4, matrix products, half_tdot(): lax.dot_general(left, right, (((0,), (0,)), ((), ())), preferred_element_...  39.6 us
    dot_general x4, matrix products, half_dot(): return jnp.dot(left, right, preferred_element_type=jnp.float32)  38.5 us
  transfers between devices with their start and end apart: 7, of which 4 were waited for; matrix products, arithmetic and copies ran while one was open for 12% of the time, Pallas kernels for 0%

commit v1 on v0

--- a/solution.py
+++ b/solution.py
@@ -191,7 +191,7 @@
     counts_f = counts.astype(jnp.float32)
     normed_low = jnp.log1p(counts_f * scale[:, None]).astype(jnp.bfloat16)
     partial_embed = half_ntdot(normed_low, emb_weight)
-    embedded = lax.psum(partial_embed, "genes")
+    embedded = jnp.sum(lax.all_gather(partial_embed, "genes"), axis=0)
     mixed_low, diverge, kept = bottleneck_forward(
         embedded, noise, ln_gain, ln_bias, lat_weight, lat_bias, up_weight, tables
     )

time: 963 us -> 998 us (1.036)
  waiting for transfers between devices: 608 us -> 628 us
  other arithmetic: 10.6 us -> 25.1 us
    all_gather x0 -> x1, waiting for transfers between devices: none -> 87.5 us  [on_device(): embedded = jnp.sum(lax.all_gather(partial_embed, 'genes'), axis=0)]
    psum x1 -> x0, waiting for transfers between devices: 67 us -> none  [on_device(): embedded = lax.psum(partial_embed, 'genes')]
    reduce_sum x0 -> x1, other arithmetic: none -> 10.4 us  [on_device(): embedded = jnp.sum(lax.all_gather(partial_embed, 'genes'), axis=0)]
where the time goes in v1:
time: 998 us; the launch traced here: 992 us
  waiting for transfers between devices  628 us (63%)
  blocking collectives  155 us (16%)
  matrix products  151 us (15%)
  other arithmetic  25.1 us (3%)
  between operations  18.8 us (2%)
  local copies, waits for them, and re-layouts  13.8 us (1%)
    reduce_scatter x1, waiting for transfers between devices, on_device(): lax.psum_scatter(emb_grad, 'cells', scatter_dimension=0, tiled=True)  231 us
    reduce_scatter x1, waiting for transfers between devices, on_device(): lax.psum_scatter(dec_grad, 'cells', scatter_dimension=0, tiled=True)  230 us
    all_gather x1, waiting for transfers between devices, on_device(): embedded = jnp.sum(lax.all_gather(partial_embed, 'genes'), axis=0)  87.5 us
    reduce_scatter x1, waiting for transfers between devices, on_device(): lax.psum_scatter(latw_grad, 'cells', scatter_dimension=0, tiled=True)  79.5 us
    psum x1, blocking collectives, on_device(): mixed_grad = lax.psum(partial_mixed, 'genes').astype(jnp.bfloat16)  76.8 us
    dot_general x4, matrix products, half_ntdot(): lax.dot_general(left, right, (((1,), (1,)), ((), ())), preferred_element_...  40.2 us
    dot_general x4, matrix products, half_tdot(): lax.dot_general(left, right, (((0,), (0,)), ((), ())), preferred_element_...  39.8 us
    dot_general x4, matrix products, half_dot(): return jnp.dot(left, right, preferred_element_type=jnp.float32)  38.5 us
  transfers between devices with their start and end apart: 7, of which 4 were waited for; matrix products, arithmetic and copies ran while one was open for 12% of the time, Pallas kernels for 0%

profile of v1, /device:TPU:0, one launch (start us, length us, event | category | flops | bytes accessed | tf_op | source)
XLA Modules:
  0.0 992.1 jit_solution(17668735077179433084)
XLA Ops:
  7.2 0.8 convert_element_type.56
  8.1 0.7 broadcast_multiply_fusion
  8.8 0.8 reduce-window.8
  9.7 0.2 select_reduce_fusion.1
  9.8 23.1 %all-reduce.4 = (f32[3]{0:T(128)S(1)}, f32[3]{0:T(128)S(1)}) all-reduce(f32[3]{0:T(128)S(1)} %get-tuple-element.17, f32[3]{0:T(128)S(1)} %get-tuple-element.16), channel_id=1, replica_groups=mesh['cells'=8,'genes'=4] {'cells'}, use_global_device_ids=true, to_apply=%region_3.4 | all-reduce | flops 6 | bytes 48 | tf_op jit(solution)/shard_map/psum | solution.py:181
  33.0 0.6 fusion.62
  33.7 0.7 convert_divide_fusion
  34.4 14.0 %fusion.1 = f32[1024,1024]{1,0:T(8,128)} fusion(bf16[1024,3375]{0,1:T(8,128)(2,1)} %param.22, bf16[1024,3375]{0,1:T(8,128)(2,1)} %param.16, f32[1024]{0:T(1024)S(1)} %convert_divide_fusion), kind=kOutput, calls=%fused_computation.5 | convolution fusion | flops 7088256000 | bytes 18022400 | tf_op jit(solution)/shard_map/dot_general | solution.py:36
  49.1 14.3 %fusion.64 = f32[1024,1024]{1,0:T(8,128)} fusion(bf16[1024,3375]{0,1:T(8,128)(2,1)} %param.31, bf16[1024,3375]{0,1:T(8,128)(2,1)} %param.28), kind=kOutput, calls=%fused_computation.101 | convolution fusion | flops 7077888000 | bytes 18018304 | tf_op jit(solution)/shard_map/dot_general | solution.py:36
  64.3 87.5 %all-gather.3.cloned.1.call-done = f32[4096,1024]{1,0:T(8,128)} async-done(((f32[1024,1024]{1,0:T(8,128)}), f32[4096,1024]{1,0:T(8,128)}) %all-gather.3.cloned.1.call-update) | async-done | bytes 16777232 | tf_op jit(solution)/shard_map/all_gather | solution.py:194
  151.8 10.4 %reduce_sum.175 = f32[1024,1024]{1,0:T(8,128)} reduce(f32[4,1024,1024]{2,1,0:T(8,128)} %bitcast.32, f32[]{:T(128)} %constant.22.clone.1), dimensions={0}, to_apply=%region_7.8 | reduce | flops 3145728 | bytes 20971524 | tf_op jit(solution)/shard_map/reduce_sum | solution.py:194
  162.1 6.6 reduce.1
  168.8 2.9 multiply_reduce_fusion.2
  171.7 0.5 copy-done.4
  172.2 2.5 broadcast_add_fusion
  174.7 1.9 convolution_multiply_fusion.1
  176.6 2.0 fusion.63
  178.6 1.8 fusion.55
  180.4 1.9 fusion.41
  182.3 1.3 copy-done.10
  183.6 3.2 multiply_reduce_fusion.4
  186.8 21.4 %psum.31 = f32[512]{0:T(512)S(1)} all-reduce(f32[512]{0:T(512)S(1)} %multiply_reduce_fusion.4), channel_id=1, replica_groups=mesh['cells'=8,'genes'=4] {'cells'}, use_global_device_ids=true, to_apply=%region_15.16 | all-reduce | flops 512 | bytes 4096 | tf_op jit(solution)/shard_map/psum | solution.py:198
  208.2 0.6 maximum_reduce_fusion
  208.8 2.0 fusion.36
  210.8 1.5 convolution_negate_fusion
  212.3 2.3 convolution_add_fusion
  214.7 2.2 multiply_reduce_fusion.5
  217.0 1.4 fusion.26
  218.4 1.3 fusion.23
  219.6 1.2 multiply_add_fusion.1
  220.9 1.7 fusion.31
  222.6 0.8 copy.45
  223.5 76.8 %all-reduce.6 = bf16[1024,1024]{1,0:T(8,128)(2,1)} all-reduce(f32[1024,1024]{1,0:T(8,128)} %fusion.64), channel_id=1, replica_groups=mesh['cells'=8,'genes'=4] {'genes'}, use_global_device_ids=true, to_apply=%region_10.11 | all-reduce | flops 1048576 | bytes 6291456 | tf_op jit(solution)/shard_map/psum | solution.py:206
  300.3 0.8 copy.43
  301.2 7.7 fusion.6
  308.9 1.0 copy-done.20
  309.9 2.7 fusion.66
  312.7 1.8 fusion.40
  314.5 6.0 add_convert_fusion.1
  320.6 1.0 copy-done.11
  321.5 4.7 fusion.37
  326.3 0.3 reduce-scatter.11.cloned.1.call-start
  326.5 8.3 multiply_reduce_fusion
  334.8 19.0 %fusion = f32[1024,3375]{0,1:T(8,128)} fusion(bf16[1024,3375]{0,1:T(8,128)(2,1)} %param.16, f32[1024]{0:T(1024)S(1)} %convert_divide_fusion, f32[1024,1024]{1,0:T(8,128)} %get-tuple-element.40, f32[1024,1024]{1,0:T(8,128)S(1)} %copy-done.6, f32[1024]{0:T(1024)S(1)} %get-tuple-element.43, f32[1024]{0:T(1024)S(1)} %get-tuple-element.44, ...), kind=kOutput, calls=%fused_computation.4 | convolution fusion | flops 7096644608 | bytes 29149184 | tf_op jit(solution)/shard_map/dot_general | solution.py:30
  353.8 0.3 reduce-scatter.17.cloned.1.call-start
  354.1 0.9 copy-done.15
  355.0 0.3 copy-done.21
  355.4 3.6 add_convert_fusion
  359.0 1.3 copy-done.22
  360.3 13.4 %fusion.65 = f32[1024,3375]{0,1:T(8,128)} fusion(bf16[1024,1024]{1,0:T(8,128)(2,1)S(1)} %add_convert_fusion, bf16[1024,3375]{0,1:T(8,128)(2,1)} %param.31), kind=kOutput, calls=%fused_computation.102 | convolution fusion | flops 7077888000 | bytes 22833152 | tf_op jit(solution)/shard_map/dot_general | solution.py:30
  373.7 0.6 copy-done.19
  374.4 0.6 dynamic-slice
  375.6 0.4 convert_reduce_fusion
  376.0 33.6 %all-reduce.3 = (f32[1024]{0:T(1024)S(1)}, f32[1024]{0:T(1024)S(1)}, f32[1024]{0:T(1024)S(1)}) all-reduce(f32[1024]{0:T(1024)S(1)} %get-tuple-element.12, f32[1024]{0:T(1024)S(1)} %get-tuple-element.15, f32[1024]{0:T(1024)S(1)} %convert_reduce_fusion), channel_id=4, replica_groups=mesh['cells'=8,'genes'=4] {'cells'}, use_global_device_ids=true, to_apply=%region_22.23.clone | all-reduce | flops 3072 | bytes 24576
  409.6 0.6 dynamic-slice.1
  410.2 0.6 dynamic-slice.3
  410.8 0.6 dynamic-slice.5
  412.0 12.2 %convolution_convert_fusion = bf16[1024,3375]{0,1:T(8,128)(2,1)} fusion(bf16[1024,1024]{1,0:T(8,128)(2,1)} %copy-done.22, bf16[1024,3375]{0,1:T(8,128)(2,1)} %param.28), kind=kOutput, calls=%fused_computation.3 | convolution fusion | flops 7081344000 | bytes 15921152 | tf_op jit(solution)/shard_map/dot_general | solution.py:26
  424.2 16.2 %divide_convert_fusion = bf16[1024,3375]{0,1:T(8,128)(2,1)} fusion(bf16[1024,3375]{0,1:T(8,128)(2,1)} %param.16, bf16[1024,3375]{0,1:T(8,128)(2,1)} %param.22, f32[1024]{0:T(1024)S(1)} %convert_divide_fusion, f32[1024,1024]{1,0:T(8,128)S(1)} %copy-done.23, f32[1024,1024]{1,0:T(8,128)S(1)} %copy-done.7, f32[1024]{0:T(1024)S(1)} %get-tuple-element.43, ...), kind=kOutput, calls=%fused_computation | convolution fusion | flops 7107012608 | bytes 29149184 | tf_op jit(solution)/shard_map/dot_general | solution.py:26
  440.4 1.4 copy.46
  441.8 1.4 copy.44
  443.2 79.5 %reduce-scatter.13.cloned.1.call-done = f32[128,1024]{1,0:T(8,128)} async-done(((f32[1024,1024]{1,0:T(8,128)}), f32[128,1024]{1,0:T(8,128)}) %reduce-scatter.13.cloned.1.call-update) | async-done | bytes 524304 | tf_op jit(solution)/shard_map/reduce_scatter | solution.py:219
  522.7 230.7 %reduce-scatter.11.cloned.1.call-done = f32[128,3375]{0,1:T(8,128)} async-done(((f32[1024,3375]{0,1:T(8,128)}), f32[128,3375]{0,1:T(8,128)}) %reduce-scatter.11.cloned.1.call-update) | async-done | bytes 1728016 | tf_op jit(solution)/shard_map/reduce_scatter | solution.py:217
  753.4 230.2 %reduce-scatter.17.cloned.1.call-done = f32[128,3375]{0,1:T(8,128)} async-done(((f32[1024,3375]{0,1:T(8,128)}), f32[128,3375]{0,1:T(8,128)}) %reduce-scatter.17.cloned.1.call-update) | async-done | bytes 1728016 | tf_op jit(solution)/shard_map/reduce_scatter | solution.py:218
  (67 shorter events, 0.9 us)
Async XLA Ops:
  7.2 164.5 %copy-start = (bf16[1024,1024]{1,0:T(8,128)(2,1)S(1)}, bf16[1024,1024]{1,0:T(8,128)(2,1)}, u32[]{:S(2)}) copy-start(bf16[1024,1024]{1,0:T(8,128)(2,1)} %param.25) | copy-start | bytes 6291460
  7.2 144.6 %all-gather.3.cloned.1.call-start = ((), (), s32[]{:S(2)}) async-start(), calls=%async_computation.10 | async-start | bytes 20971520 | tf_op jit(solution)/shard_map/all_gather | solution.py:194
  48.4 392.0 %reduce-scatter.21.cloned.1.call-start = ((), (), s32[]{:S(2)}) async-start(), calls=%async_computation.12 | async-start | bytes 294912
  49.1 15.0 %copy-start.13 = (f32[512,16]{0,1:T(8,128)S(1)}, f32[512,16]{0,1:T(8,128)}, u32[]{:S(2)}) copy-start(f32[512,16]{0,1:T(8,128)} %param.30) | copy-start | bytes 98308
  49.1 15.0 %copy-start.14 = (f32[512,16]{0,1:T(8,128)S(1)}, f32[512,16]{0,1:T(8,128)}, u32[]{:S(2)}) copy-start(f32[512,16]{0,1:T(8,128)} %param.29) | copy-start | bytes 98308
  168.7 3.0 copy-start.16
  168.7 3.0 copy-start.17
  168.7 3.0 copy-start.18
  168.8 3.5 copy-start.4
  174.7 7.6 copy-start.2
  180.4 1.9 copy-start.9
  182.3 1.3 copy-start.10
  208.2 2.7 copy-start.3
  223.4 218.4 %reduce-scatter.19.cloned.1.call-start = ((), (), s32[]{:S(2)}) async-start(), calls=%async_computation.11 | async-start | bytes 294912
  301.2 142.1 %reduce-scatter.15.cloned.1.call-start = ((), (), s32[]{:S(2)}) async-start(), calls=%async_computation.8 | async-start | bytes 2359296 | tf_op jit(solution)/shard_map/reduce_scatter | solution.py:220
  301.2 8.7 copy-start.8
  308.9 1.0 copy-start.20
  312.6 210.1 %reduce-scatter.13.cloned.1.call-start = ((), (), s32[]{:S(2)}) async-start(), calls=%async_computation.7 | async-start | bytes 4718592 | tf_op jit(solution)/shard_map/reduce_scatter | solution.py:219
  314.5 7.0 copy-start.5
  320.6 1.0 copy-start.11
  326.3 427.1 %reduce-scatter.11.cloned.1.call-start = ((), (), s32[]{:S(2)}) async-start(), calls=%async_computation.6 | async-start | bytes 15556608 | tf_op jit(solution)/shard_map/reduce_scatter | solution.py:217
  326.5 8.3 copy-start.6
  353.8 1.2 copy-start.15
  353.8 1.5 copy-start.21
  353.8 629.8 %reduce-scatter.17.cloned.1.call-start = ((), (), s32[]{:S(2)}) async-start(), calls=%async_computation.9 | async-start | bytes 15556608 | tf_op jit(solution)/shard_map/reduce_scatter | solution.py:218
  359.0 1.3 copy-start.22
  373.7 0.7 copy-start.19
  373.7 1.9 copy-start.12
  412.0 12.2 %copy-start.7 = (f32[1024,1024]{1,0:T(8,128)S(1)}, f32[1024,1024]{1,0:T(8,128)}, u32[]{:S(2)}) copy-start(f32[1024,1024]{1,0:T(8,128)} %reduce_sum.175) | copy-start | bytes 12582916
  412.0 12.2 %copy-start.23 = (f32[1024,1024]{1,0:T(8,128)S(1)}, f32[1024,1024]{1,0:T(8,128)}, u32[]{:S(2)}) copy-start(f32[1024,1024]{1,0:T(8,128)} %get-tuple-element.40) | copy-start | bytes 12582916
  424.2 559.4 %copy-start.1 = (bf16[1024,1024]{1,0:T(8,128)(2,1)S(1)}, bf16[1024,1024]{1,0:T(8,128)(2,1)}, u32[]{:S(2)}) copy-start(bf16[1024,1024]{1,0:T(8,128)(2,1)} %param.25) | copy-start | bytes 6291460
Sparse Core Ops, SparseCore 0:
  48.5 103.1 all-gather.2
  223.6 58.3 reduce-scatter.20
  301.3 58.2 reduce-scatter.18
  363.5 67.6 reduce-scatter.14
  435.3 87.3 reduce-scatter.12
  526.6 226.6 reduce-scatter.10
  757.5 226.0 reduce-scatter.16
